TPU v7x, 256 devices: a whole 4x4x8 slice. The times are simulated.
256 devices in a mesh: seq: 32 (over x, z), ch: 8 (over y, core).
Axes of the slice: x: 4, y: 4, z: 8, core: 2. Of those that a mesh axis runs over, the one named last changes fastest.
Arguments:
- out_gate: bfloat16 [12288, 4096], P('seq', 'ch'), may hold values from -6 to 6
- in_gate: bfloat16 [12288, 4096], P('seq', 'ch'), may hold values from -6 to 6
- values: bfloat16 [12288, 4096], P('seq', 'ch'), may hold values from -6 to 6
- short_filter: float32 [3, 3, 4096], P(None, None, 'ch'), may hold values from -3 to 3
- long_filter: float32 [12288, 4096], P('seq', 'ch'), may hold values from -1.5 to 1.5
- skip_gain: float32 [4096], P('ch'), may hold values from -4 to 4
- out_weight: bfloat16 [4096, 4096], P(None, 'ch'), may hold values from -0.09375 to 0.09375
Outputs:
- projected: bfloat16 [12288, 4096], P('seq', 'ch')
All inputs are finite; a program needn't handle non-finite values.
Results may differ from a plain program's by a relative error of at most 0.0049.
Values may be sent and summed in bfloat16 or wider, within the bound.
A program may use at most 128 MiB of HBM per device.

v0:
```python
import math
import jax
import jax.numpy as jnp
import numpy as np
from jax import lax
from jax.sharding import PartitionSpec as P

high = lax.Precision.HIGH


def contract(pattern, first_op, second_op):
    return jnp.einsum(
        pattern, first_op, second_op, precision=high, preferred_element_type=jnp.float32
    )


def tables(seq_len, inner):
    total = 2 * seq_len
    outer = total // inner
    half = seq_len // inner
    k1 = np.arange(outer)[:, None]
    n1 = np.arange(half)[None, :]
    a1 = 2.0 * np.pi * (k1 * n1 % outer) / outer
    n2 = np.arange(inner)[None, :]
    at = 2.0 * np.pi * (k1 * n2 % total) / total
    m2 = np.arange(inner)
    a2 = 2.0 * np.pi * (m2[:, None] * m2[None, :] % inner) / inner
    f32 = lambda v: jnp.asarray(v, jnp.float32)
    return dict(
        c1=f32(np.cos(a1)),
        s1=f32(np.sin(a1)),
        tc=f32(np.cos(at)[:, :, None]),
        ts=f32(np.sin(at)[:, :, None]),
        c2=f32(np.cos(a2)),
        s2=f32(np.sin(a2)),
        c1i=f32(np.cos(a1).T / total),
        s1i=f32(np.sin(a1).T / total),
    )


def forward(signal, tb):
    br = contract("kn,nmc->kmc", tb["c1"], signal)
    bi = -contract("kn,nmc->kmc", tb["s1"], signal)
    tr, ti = (tb["tc"], -tb["ts"])
    br, bi = (br * tr - bi * ti, br * ti + bi * tr)
    xr = contract("kmc,mj->kjc", br, tb["c2"]) + contract("kmc,mj->kjc", bi, tb["s2"])
    xi = contract("kmc,mj->kjc", bi, tb["c2"]) - contract("kmc,mj->kjc", br, tb["s2"])
    return (xr, xi)


def inverse(yr, yi, tb):
    zr = contract("kjc,jm->kmc", yr, tb["c2"]) - contract("kjc,jm->kmc", yi, tb["s2"])
    zi = contract("kjc,jm->kmc", yr, tb["s2"]) + contract("kjc,jm->kmc", yi, tb["c2"])
    tc, ts = (tb["tc"], tb["ts"])
    zr, zi = (zr * tc - zi * ts, zr * ts + zi * tc)
    return contract("nk,kmc->nmc", tb["c1i"], zr) - contract("nk,kmc->nmc", tb["s1i"], zi)


def long_conv(mixed_in, long_filter, inner):
    seq_len, width = mixed_in.shape
    half = seq_len // inner
    tb = tables(seq_len, inner)
    xr, xi = forward(mixed_in.reshape(half, inner, width), tb)
    hr, hi = forward(long_filter.reshape(half, inner, width), tb)
    yr = xr * hr - xi * hi
    yi = xr * hi + xi * hr
    return inverse(yr, yi, tb).reshape(seq_len, width)


def short_conv(signal, taps):
    tap_count = taps.shape[0]
    widened = jnp.pad(signal, ((tap_count - 1, 0), (0, 0)))
    seq_len = signal.shape[0]
    summed = taps[0] * widened[tap_count - 1 :]
    for offset in range(1, tap_count):
        start = tap_count - 1 - offset
        summed = summed + taps[offset] * widened[start : start + seq_len]
    return summed


def on_device(out_gate, in_gate, values, short_filter, long_filter, skip_gain, out_weight):
    seq_count = lax.axis_size("seq")
    seq_index = lax.axis_index("seq")
    width = out_gate.shape[1] // seq_count
    stacked = jnp.stack([out_gate, in_gate, values])
    spread = lax.all_to_all(stacked, "seq", split_axis=2, concat_axis=1, tiled=True)
    filt = lax.all_to_all(long_filter, "seq", split_axis=1, concat_axis=0, tiled=True)
    start = seq_index * width
    taps = lax.dynamic_slice_in_dim(short_filter, start, width, axis=2)
    gain = lax.dynamic_slice_in_dim(skip_gain, start, width, axis=0)
    spread = spread.astype(jnp.float32)
    gate_late = short_conv(spread[0], taps[0])
    mixed_in = short_conv(spread[1], taps[1]) * short_conv(spread[2], taps[2])
    long_out = long_conv(mixed_in, filt, 192)
    filtered = long_out + gain * mixed_in
    mixed = (gate_late * filtered).astype(jnp.bfloat16)
    mixed = lax.all_to_all(mixed, "seq", split_axis=0, concat_axis=1, tiled=True)
    summed = jnp.dot(
        lax.all_gather(mixed, "ch", axis=1, tiled=True),
        out_weight,
        preferred_element_type=jnp.float32,
    )
    return summed.astype(jnp.bfloat16)


def solution(mesh):
    return jax.shard_map(
        on_device,
        mesh=mesh,
        in_specs=(
            P("seq", "ch"),
            P("seq", "ch"),
            P("seq", "ch"),
            P(None, None, "ch"),
            P("seq", "ch"),
            P("ch"),
            P(None, "ch"),
        ),
        out_specs=P("seq", "ch"),
        check_vma=False,
    )
```

profile of v0, /device:TPU:1, one launch (start us, length us, event | category | flops | bytes accessed | tf_op | source)
XLA Modules:
  0.0 170.3 jit_solution(440597330835324851)
XLA Ops:
  6.5 2.4 %copy.57 = f32[384,512]{0,1:T(8,128)} copy(f32[384,512]{1,0:T(8,128)} %param.19) | data formatting | bytes 1572864 | tf_op args[4]
  8.9 11.9 %all-to-all-start.1 = ((f32[384,32,16]{0,2,1:T(8,128)}), f32[384,32,16]{0,2,1:T(8,128)S(1)}, u32[]{:S(2)}, u32[]{:S(2)}) async-start(f32[384,32,16]{0,2,1:T(8,128)} %bitcast.20), calls=%async_computation.1 | async-start | bytes 1572864 | tf_op jit(solution)/shard_map/all_to_all | solution.py:87
  21.0 2.3 %copy.50 = bf16[3,384,512]{1,0,2:T(4,128)(2,1)} copy(bf16[3,384,512]{2,1,0:T(8,128)(2,1)S(1)} %pad_maximum_fusion) | data formatting | bytes 2359296 | tf_op jit(solution)/shard_map/stack | solution.py:85
  23.3 16.8 %all-to-all-done.1 = f32[384,32,16]{0,2,1:T(8,128)S(1)} async-done(((f32[384,32,16]{0,2,1:T(8,128)}), f32[384,32,16]{0,2,1:T(8,128)S(1)}, u32[]{:S(2)}, u32[]{:S(2)}) %all-to-all-start.1) | async-done | bytes 786464 | tf_op jit(solution)/shard_map/all_to_all | solution.py:87
  40.1 8.4 %all-to-all-start = ((bf16[3,384,512]{1,0,2:T(4,128)(2,1)}), bf16[3,384,512]{1,0,2:T(4,128)(2,1)S(1)}, u32[]{:S(2)}, u32[]{:S(2)}) async-start(bf16[3,384,512]{1,0,2:T(4,128)(2,1)} %copy.50), calls=%async_computation | async-start | bytes 3145728 | tf_op jit(solution)/shard_map/all_to_all | solution.py:86
  49.2 0.9 fusion.31
  50.1 1.1 copy.58
  51.3 1.4 reshape.45
  52.7 1.4 convolution_negate_fusion
  54.1 1.4 fusion.39
  55.6 1.0 fusion.23
  56.6 1.0 fusion.22
  57.5 2.1 %convolution_subtract_fusion = f32[128,16,192]{0,2,1:T(8,128)} fusion(f32[128,16,192]{0,2,1:T(8,128)S(1)} %fusion.23, f32[192,192,1]{0,1,2:T(8,128)S(1)} %copy-done.2, f32[128,192,16]{0,1,2:T(8,128)S(1)} %convolution_negate_fusion, f32[128,192,16]{0,1,2:T(8,128)S(1)} %fusion.39, f32[128,192]{0,1:T(8,128)S(1)} %copy-done.5, f32[128,192]{0,1:T(8,128)S(1)} %copy-done), kind=kOutput, calls=%fused_computation.28 | convolution fusion | flops 454557696 | bytes 6635520 | tf_op jit(solution)/shard_map/kmc,mj->kjc/dot_general | solution.py:12
  59.7 2.1 %convolution_add_fusion = f32[128,16,192]{0,2,1:T(8,128)} fusion(f32[128,16,192]{0,2,1:T(8,128)S(1)} %fusion.22, f32[192,192,1]{0,1,2:T(8,128)S(1)} %copy-done.2, f32[128,192,16]{0,1,2:T(8,128)S(1)} %convolution_negate_fusion, f32[128,192,16]{0,1,2:T(8,128)S(1)} %fusion.39, f32[128,192]{0,1:T(8,128)S(1)} %copy-done.5, f32[128,192]{0,1:T(8,128)S(1)} %copy-done), kind=kOutput, calls=%fused_computation.30 | convolution fusion | flops 454557696 | bytes 6635520 | tf_op jit(solution)/shard_map/kmc,mj->kjc/dot_general | solution.py:12
  61.8 23.4 %all-to-all-done = bf16[3,384,512]{1,0,2:T(4,128)(2,1)S(1)} async-done(((bf16[3,384,512]{1,0,2:T(4,128)(2,1)}), bf16[3,384,512]{1,0,2:T(4,128)(2,1)S(1)}, u32[]{:S(2)}, u32[]{:S(2)}) %all-to-all-start) | async-done | bytes 1179680 | tf_op jit(solution)/shard_map/all_to_all | solution.py:86
  85.9 0.9 add_multiply_fusion
  87.2 1.4 convolution_negate_fusion.1
  88.7 1.4 fusion.38
  90.1 1.2 fusion.24
  91.3 1.0 fusion.28
  92.3 1.0 convolution_add_fusion.1
  94.1 1.5 multiply_subtract_fusion
  97.3 0.9 copy.66
  98.2 0.9 fusion.16
  99.2 1.2 subtract_bitcast_fusion.1
  100.5 1.5 fusion.10
  102.0 1.6 subtract_bitcast_fusion
  103.6 1.7 %copy.61 = f32[64,192,16]{1,0,2:T(8,128)} copy(f32[64,192,16]{0,2,1:T(8,128)S(1)} %subtract_bitcast_fusion) | data formatting | bytes 1572864 | tf_op jit(solution)/shard_map/sub | solution.py:56
  105.4 1.7 reshape.46
  107.6 18.3 %all_to_all.44 = bf16[32,384,16]{1,2,0:T(8,128)(2,1)} all-to-all(bf16[32,384,16]{1,2,0:T(8,128)(2,1)S(1)} %bitcast.133), channel_id=1, replica_groups=mesh['seq'=32,'ch'=8] {'seq'}, dimensions={0} | all-to-all | bytes 786432 | tf_op jit(solution)/shard_map/all_to_all | solution.py:97
  126.0 31.7 %all-gather.2.cloned.1.call-done = bf16[384,4096]{0,1:T(8,128)(2,1)} async-done(((bf16[384,512]{0,1:T(8,128)(2,1)}), bf16[384,4096]{0,1:T(8,128)(2,1)}) %all-gather.2.cloned.1.call-update) | async-done | bytes 3145744 | tf_op jit(solution)/shard_map/all_gather | solution.py:99
  157.7 5.7 %convolution_convert_fusion = bf16[384,512]{1,0:T(8,128)(2,1)} fusion(bf16[384,4096]{0,1:T(8,128)(2,1)} %all-gather.2.cloned.1.call-done, bf16[4096,512]{1,0:T(8,128)(2,1)} %param.21), kind=kOutput, calls=%fused_computation.32 | convolution fusion | flops 1610809344 | bytes 7733248 | tf_op jit(solution)/shard_map/dot_general | solution.py:98
  (44 shorter events, 5.1 us)
Async XLA Ops:
  6.5 14.3 %copy-start.7 = (bf16[384,512]{1,0:T(8,128)(2,1)S(1)}, bf16[384,512]{1,0:T(8,128)(2,1)}, u32[]{:S(2)}) copy-start(bf16[384,512]{1,0:T(8,128)(2,1)} %param.17) | copy-start | bytes 1179652
  6.5 14.3 %copy-start.8 = (bf16[384,512]{1,0:T(8,128)(2,1)S(1)}, bf16[384,512]{1,0:T(8,128)(2,1)}, u32[]{:S(2)}) copy-start(bf16[384,512]{1,0:T(8,128)(2,1)} %param.16) | copy-start | bytes 1179652
  6.5 14.3 %copy-start.9 = (bf16[384,512]{1,0:T(8,128)(2,1)S(1)}, bf16[384,512]{1,0:T(8,128)(2,1)}, u32[]{:S(2)}) copy-start(bf16[384,512]{1,0:T(8,128)(2,1)} %param.15) | copy-start | bytes 1179652
  8.9 31.1 %all-to-all-start.1 = ((f32[384,32,16]{0,2,1:T(8,128)}), f32[384,32,16]{0,2,1:T(8,128)S(1)}, u32[]{:S(2)}, u32[]{:S(2)}) async-start(f32[384,32,16]{0,2,1:T(8,128)} %bitcast.20), calls=%async_computation.1 | async-start | bytes 1572864 | tf_op jit(solution)/shard_map/all_to_all | solution.py:87
  40.1 45.2 %all-to-all-start = ((bf16[3,384,512]{1,0,2:T(4,128)(2,1)}), bf16[3,384,512]{1,0,2:T(4,128)(2,1)S(1)}, u32[]{:S(2)}, u32[]{:S(2)}) async-start(bf16[3,384,512]{1,0,2:T(4,128)(2,1)} %copy.50), calls=%async_computation | async-start | bytes 3145728 | tf_op jit(solution)/shard_map/all_to_all | solution.py:86
  48.4 109.3 %all-gather.2.cloned.1.call-start = ((), (), s32[]{:S(2)}) async-start(), calls=%async_computation.3 | async-start | bytes 3538944 | tf_op jit(solution)/shard_map/all_gather | solution.py:99
  50.1 2.5 %copy-start.11 = (f32[128,64,1]{0,1,2:T(8,128)S(1)}, f32[128,64,1]{0,1,2:T(8,128)}, u32[]{:S(2)}) copy-start(f32[128,64,1]{0,1,2:T(8,128)} %constant.49) | copy-start | bytes 98308
  52.7 1.4 copy-start.10
  54.1 1.5 copy-start
  54.1 1.5 copy-start.1
  54.1 1.5 copy-start.5
  56.6 1.0 copy-start.2
  92.2 1.4 copy-start.3
  92.2 1.9 %copy-start.4 = (f32[128,16,192]{0,2,1:T(8,128)S(1)}, f32[128,16,192]{0,2,1:T(8,128)}, u32[]{:S(2)}) copy-start(f32[128,16,192]{0,2,1:T(8,128)} %convolution_add_fusion) | copy-start | bytes 4718596
  98.2 0.9 copy-start.12
  99.2 1.3 copy-start.14
  100.5 1.6 copy-start.13
  105.4 1.7 copy-start.6
Sparse Core Ops, SparseCore 0:
  126.1 31.5 all-gather.1
where the time goes:
time: 171 us; the launch traced here: 170 us
  waiting for transfers between devices  71.9 us (42%)
  matrix products  29.1 us (17%)
  starting transfers between devices  20.3 us (12%)
  blocking collectives  18.3 us (11%)
  local copies, waits for them, and re-layouts  15.1 us (9%)
  between operations  13.8 us (8%)
  other arithmetic  1.73 us (1%)
    all_gather x1, waiting for transfers between devices, on_device(): lax.all_gather(mixed, 'ch', axis=1, tiled=True)  31.7 us
    all_to_all x1, waiting for transfers between devices, on_device(): lax.all_to_all(stacked, 'seq', split_axis=2, concat_axis=1, tiled=True)  23.4 us
    dot_general x18, matrix products, contract(): jnp.einsum(pattern, first_op, second_op, precision=high, preferred_elemen...  23.4 us
    all_to_all x1, blocking collectives, on_device(): lax.all_to_all(mixed, 'seq', split_axis=0, concat_axis=1, tiled=True)  18.3 us
    all_to_all x1, waiting for transfers between devices, on_device(): lax.all_to_all(long_filter, 'seq', split_axis=1, concat_axis=0, tiled=True)  16.8 us
    all_to_all x1, starting transfers between devices, on_device(): lax.all_to_all(long_filter, 'seq', split_axis=1, concat_axis=0, tiled=True)  11.9 us
    all_to_all x1, starting transfers between devices, on_device(): lax.all_to_all(stacked, 'seq', split_axis=2, concat_axis=1, tiled=True)  8.36 us
    dot_general x1, matrix products, on_device(): jnp.dot(lax.all_gather(mixed, 'ch', axis=1, tiled=True), out_weight, pref...  5.7 us
  transfers between devices with their start and end apart: 3, of which 3 were waited for; matrix products, arithmetic and copies ran while one was open for 9% of the time, Pallas kernels for 0%

commit v1 on v0

--- a/solution.py
+++ b/solution.py
@@ -6,6 +6,27 @@
 from jax.sharding import PartitionSpec as P
 
 high = lax.Precision.HIGH
+
+
+def gather_around(x, axis, dim):
+    peers, here, rows = (lax.axis_size(axis), lax.axis_index(axis), x.shape[dim])
+    ahead = [(i, (i + 1) % peers) for i in range(peers)]
+    backward = [(i, (i - 1) % peers) for i in range(peers)]
+    result = jnp.zeros((*x.shape[:dim], peers * rows, *x.shape[dim + 1 :]), x.dtype)
+    result = lax.dynamic_update_slice_in_dim(result, x, here * rows, axis=dim)
+    from_left = from_right = x
+    half = peers // 2
+    for step in range(1, half + 1):
+        from_left = lax.ppermute(from_left, axis, ahead)
+        result = lax.dynamic_update_slice_in_dim(
+            result, from_left, (here - step) % peers * rows, axis=dim
+        )
+        if step < peers - half:
+            from_right = lax.ppermute(from_right, axis, backward)
+            result = lax.dynamic_update_slice_in_dim(
+                result, from_right, (here + step) % peers * rows, axis=dim
+            )
+    return result
 
 
 def contract(pattern, first_op, second_op):
@@ -95,11 +116,7 @@
     filtered = long_out + gain * mixed_in
     mixed = (gate_late * filtered).astype(jnp.bfloat16)
     mixed = lax.all_to_all(mixed, "seq", split_axis=0, concat_axis=1, tiled=True)
-    summed = jnp.dot(
-        lax.all_gather(mixed, "ch", axis=1, tiled=True),
-        out_weight,
-        preferred_element_type=jnp.float32,
-    )
+    summed = jnp.dot(gather_around(mixed, "ch", 1), out_weight, preferred_element_type=jnp.float32)
     return summed.astype(jnp.bfloat16)
 
 

time: 171 us -> 160 us (0.936)
  the two profiles are of different devices: /device:TPU:1 before, /device:TPU:32 now
where the time goes in v1:
time: 160 us; the launch traced here: 159 us
  waiting for transfers between devices  70.4 us (44%)
  matrix products  25.9 us (16%)
  starting transfers between devices  25 us (16%)
  blocking collectives  19.7 us (12%)
  local copies, waits for them, and re-layouts  16.1 us (10%)
  other arithmetic  1.73 us (1%)
    all_to_all x1, waiting for transfers between devices, on_device(): lax.all_to_all(stacked, 'seq', split_axis=2, concat_axis=1, tiled=True)  25.7 us
    ppermute x4, waiting for transfers between devices, gather_around(): from_left = lax.ppermute(from_left, axis, ahead)  23.9 us
    dot_general x18, matrix products, contract(): jnp.einsum(pattern, first_op, second_op, precision=high, preferred_elemen...  23.4 us
    all_to_all x1, waiting for transfers between devices, on_device(): lax.all_to_all(long_filter, 'seq', split_axis=1, concat_axis=0, tiled=True)  20.7 us
    all_to_all x1, blocking collectives, on_device(): lax.all_to_all(mixed, 'seq', split_axis=0, concat_axis=1, tiled=True)  19.7 us
    all_to_all x1, starting transfers between devices, on_device(): lax.all_to_all(long_filter, 'seq', split_axis=1, concat_axis=0, tiled=True)  11.2 us
    ppermute x3, starting transfers between devices, gather_around(): from_right = lax.ppermute(from_right, axis, backward)  8.87 us
    all_to_all x1, starting transfers between devices, on_device(): lax.all_to_all(stacked, 'seq', split_axis=2, concat_axis=1, tiled=True)  4.93 us
  transfers between devices with their start and end apart: 9, of which 7 were waited for; matrix products, arithmetic and copies ran while one was open for 10% of the time, Pallas kernels for 0%

profile of v1, /device:TPU:32, one launch (start us, length us, event | category | flops | bytes accessed | tf_op | source)
XLA Modules:
  0.0 159.4 jit_solution(1550677289257289783)
XLA Ops:
  0.0 2.4 %copy.57 = f32[384,512]{0,1:T(8,128)} copy(f32[384,512]{1,0:T(8,128)} %param.19) | data formatting | bytes 1572864 | tf_op args[4]
  2.4 11.2 %all-to-all-start.1 = ((f32[384,32,16]{0,2,1:T(8,128)}), f32[384,32,16]{0,2,1:T(8,128)S(1)}, u32[]{:S(2)}, u32[]{:S(2)}) async-start(f32[384,32,16]{0,2,1:T(8,128)} %bitcast.20), calls=%async_computation.1 | async-start | bytes 1572864 | tf_op jit(solution)/shard_map/all_to_all | solution.py:108
  13.8 2.3 %copy.50 = bf16[3,384,512]{1,0,2:T(4,128)(2,1)} copy(bf16[3,384,512]{2,1,0:T(8,128)(2,1)S(1)} %pad_maximum_fusion) | data formatting | bytes 2359296 | tf_op jit(solution)/shard_map/stack | solution.py:106
  16.1 20.7 %all-to-all-done.1 = f32[384,32,16]{0,2,1:T(8,128)S(1)} async-done(((f32[384,32,16]{0,2,1:T(8,128)}), f32[384,32,16]{0,2,1:T(8,128)S(1)}, u32[]{:S(2)}, u32[]{:S(2)}) %all-to-all-start.1) | async-done | bytes 786464 | tf_op jit(solution)/shard_map/all_to_all | solution.py:108
  36.8 4.9 %all-to-all-start = ((bf16[3,384,512]{1,0,2:T(4,128)(2,1)}), bf16[3,384,512]{1,0,2:T(4,128)(2,1)S(1)}, u32[]{:S(2)}, u32[]{:S(2)}) async-start(bf16[3,384,512]{1,0,2:T(4,128)(2,1)} %copy.50), calls=%async_computation | async-start | bytes 3145728 | tf_op jit(solution)/shard_map/all_to_all | solution.py:107
  43.4 1.1 copy.58
  44.5 1.4 reshape.45
  45.9 1.4 convolution_negate_fusion
  47.4 1.4 fusion.39
  50.8 2.1 %convolution_subtract_fusion = f32[128,16,192]{0,2,1:T(8,128)} fusion(f32[128,16,192]{0,2,1:T(8,128)S(1)} %fusion.23, f32[192,192,1]{0,1,2:T(8,128)S(1)} %copy-done.2, f32[128,192,16]{0,1,2:T(8,128)S(1)} %convolution_negate_fusion, f32[128,192,16]{0,1,2:T(8,128)S(1)} %fusion.39, f32[128,192]{0,1:T(8,128)S(1)} %copy-done.5, f32[128,192]{0,1:T(8,128)S(1)} %copy-done), kind=kOutput, calls=%fused_computation.28 | convolution fusion | flops 454557696 | bytes 6635520 | tf_op jit(solution)/shard_map/kmc,mj->kjc/dot_general | solution.py:33
  52.9 2.1 %convolution_add_fusion = f32[128,16,192]{0,2,1:T(8,128)} fusion(f32[128,16,192]{0,2,1:T(8,128)S(1)} %fusion.22, f32[192,192,1]{0,1,2:T(8,128)S(1)} %copy-done.2, f32[128,192,16]{0,1,2:T(8,128)S(1)} %convolution_negate_fusion, f32[128,192,16]{0,1,2:T(8,128)S(1)} %fusion.39, f32[128,192]{0,1:T(8,128)S(1)} %copy-done.5, f32[128,192]{0,1:T(8,128)S(1)} %copy-done), kind=kOutput, calls=%fused_computation.30 | convolution fusion | flops 454557696 | bytes 6635520 | tf_op jit(solution)/shard_map/kmc,mj->kjc/dot_general | solution.py:33
  55.0 25.7 %all-to-all-done = bf16[3,384,512]{1,0,2:T(4,128)(2,1)S(1)} async-done(((bf16[3,384,512]{1,0,2:T(4,128)(2,1)}), bf16[3,384,512]{1,0,2:T(4,128)(2,1)S(1)}, u32[]{:S(2)}, u32[]{:S(2)}) %all-to-all-start) | async-done | bytes 1179680 | tf_op jit(solution)/shard_map/all_to_all | solution.py:107
  82.8 1.4 convolution_negate_fusion.1
  84.2 1.4 fusion.38
  85.6 1.1 fusion.24
  86.8 1.0 fusion.28
  87.8 1.0 convolution_add_fusion.1
  89.7 1.5 multiply_subtract_fusion
  94.7 1.2 subtract_bitcast_fusion.1
  96.0 1.5 fusion.10
  97.5 1.6 subtract_bitcast_fusion
  99.1 1.7 %copy.61 = f32[64,192,16]{1,0,2:T(8,128)} copy(f32[64,192,16]{0,2,1:T(8,128)S(1)} %subtract_bitcast_fusion) | data formatting | bytes 1572864 | tf_op jit(solution)/shard_map/sub | solution.py:77
  100.9 1.9 %reshape.46 = f32[12288,16]{0,1:T(8,128)S(1)} reshape(f32[64,192,16]{1,0,2:T(8,128)} %copy.61) | data formatting | bytes 1572864 | tf_op jit(solution)/shard_map/reshape | solution.py:88
  103.3 19.7 %all_to_all.44 = bf16[32,384,16]{1,2,0:T(8,128)(2,1)S(1)} all-to-all(bf16[32,384,16]{1,2,0:T(8,128)(2,1)S(1)} %bitcast.132), channel_id=1, replica_groups=mesh['seq'=32,'ch'=8] {'seq'}, dimensions={0} | all-to-all | bytes 786432 | tf_op jit(solution)/shard_map/all_to_all | solution.py:118
  123.1 3.0 %collective-permute-start.1 = (bf16[384,512]{0,1:T(8,128)(2,1)S(1)}, bf16[384,512]{0,1:T(8,128)(2,1)S(1)}, u32[]{:S(2)}, u32[]{:S(2)}) collective-permute-start(bf16[384,512]{0,1:T(8,128)(2,1)S(1)} %bitcast.134), channel_id=1, source_target_pairs={{0,7},{1,0},{2,1},{3,2},{4,3},{5,4},{6,5},{7,6},{8,15},{9,8},{10,9... | collective-permute-start | bytes 1179656 | tf_op jit(solution)/shard_map/ppermute | solution.py:25
  126.0 5.5 %collective-permute-done = bf16[384,512]{0,1:T(8,128)(2,1)S(1)} collective-permute-done((bf16[384,512]{0,1:T(8,128)(2,1)S(1)}, bf16[384,512]{0,1:T(8,128)(2,1)S(1)}, u32[]{:S(2)}, u32[]{:S(2)}) %collective-permute-start) | collective-permute-done | bytes 393248 | tf_op jit(solution)/shard_map/ppermute | solution.py:20
  131.5 3.0 %collective-permute-start.3 = (bf16[384,512]{0,1:T(8,128)(2,1)S(1)}, bf16[384,512]{0,1:T(8,128)(2,1)S(1)}, u32[]{:S(2)}, u32[]{:S(2)}) collective-permute-start(bf16[384,512]{0,1:T(8,128)(2,1)S(1)} %collective-permute-done.1), channel_id=1, source_target_pairs={{0,7},{1,0},{2,1},{3,2},{4,3},{5,4},{6,5},{7,6},{8,15},{9,8},{10,9... | collective-permute-start | bytes 1179656 | tf_op jit(solution)/shard_map/ppermute | solution.py:25
  134.4 5.5 %collective-permute-done.2 = bf16[384,512]{0,1:T(8,128)(2,1)S(1)} collective-permute-done((bf16[384,512]{0,1:T(8,128)(2,1)S(1)}, bf16[384,512]{0,1:T(8,128)(2,1)S(1)}, u32[]{:S(2)}, u32[]{:S(2)}) %collective-permute-start.2) | collective-permute-done | bytes 393248 | tf_op jit(solution)/shard_map/ppermute | solution.py:20
  140.3 3.0 %collective-permute-start.5 = (bf16[384,512]{0,1:T(8,128)(2,1)S(1)}, bf16[384,512]{0,1:T(8,128)(2,1)S(1)}, u32[]{:S(2)}, u32[]{:S(2)}) collective-permute-start(bf16[384,512]{0,1:T(8,128)(2,1)S(1)} %collective-permute-done.3), channel_id=1, source_target_pairs={{0,7},{1,0},{2,1},{3,2},{4,3},{5,4},{6,5},{7,6},{8,15},{9,8},{10,9... | collective-permute-start | bytes 1179656 | tf_op jit(solution)/shard_map/ppermute | solution.py:25
  143.4 4.9 %collective-permute-done.4 = bf16[384,512]{0,1:T(8,128)(2,1)S(1)} collective-permute-done((bf16[384,512]{0,1:T(8,128)(2,1)S(1)}, bf16[384,512]{0,1:T(8,128)(2,1)S(1)}, u32[]{:S(2)}, u32[]{:S(2)}) %collective-permute-start.4) | collective-permute-done | bytes 393248 | tf_op jit(solution)/shard_map/ppermute | solution.py:20
  148.7 8.1 %collective-permute-done.6 = bf16[384,512]{0,1:T(8,128)(2,1)S(1)} collective-permute-done((bf16[384,512]{0,1:T(8,128)(2,1)S(1)}, bf16[384,512]{0,1:T(8,128)(2,1)S(1)}, u32[]{:S(2)}, u32[]{:S(2)}) %collective-permute-start.6) | collective-permute-done | bytes 393248 | tf_op jit(solution)/shard_map/ppermute | solution.py:20
  156.8 2.6 %convolution_convert_fusion = bf16[384,512]{1,0:T(8,128)(2,1)} fusion(bf16[384,4096]{0,1:T(8,128)(2,1)S(1)} %constant_dynamic-update-slice_fusion, bf16[4096,512]{1,0:T(8,128)(2,1)S(1)} %copy-done.15), kind=kOutput, calls=%fused_computation.32 | convolution fusion | flops 1610809344 | bytes 7733248 | tf_op jit(solution)/shard_map/dot_general | solution.py:119
  (66 shorter events, 11.5 us)
Async XLA Ops:
  0.0 13.6 %copy-start.7 = (bf16[384,512]{1,0:T(8,128)(2,1)S(1)}, bf16[384,512]{1,0:T(8,128)(2,1)}, u32[]{:S(2)}) copy-start(bf16[384,512]{1,0:T(8,128)(2,1)} %param.17) | copy-start | bytes 1179652
  0.0 13.6 %copy-start.8 = (bf16[384,512]{1,0:T(8,128)(2,1)S(1)}, bf16[384,512]{1,0:T(8,128)(2,1)}, u32[]{:S(2)}) copy-start(bf16[384,512]{1,0:T(8,128)(2,1)} %param.16) | copy-start | bytes 1179652
  0.0 13.6 %copy-start.9 = (bf16[384,512]{1,0:T(8,128)(2,1)S(1)}, bf16[384,512]{1,0:T(8,128)(2,1)}, u32[]{:S(2)}) copy-start(bf16[384,512]{1,0:T(8,128)(2,1)} %param.15) | copy-start | bytes 1179652
  2.4 34.4 %all-to-all-start.1 = ((f32[384,32,16]{0,2,1:T(8,128)}), f32[384,32,16]{0,2,1:T(8,128)S(1)}, u32[]{:S(2)}, u32[]{:S(2)}) async-start(f32[384,32,16]{0,2,1:T(8,128)} %bitcast.20), calls=%async_computation.1 | async-start | bytes 1572864 | tf_op jit(solution)/shard_map/all_to_all | solution.py:108
  36.8 44.0 %all-to-all-start = ((bf16[3,384,512]{1,0,2:T(4,128)(2,1)}), bf16[3,384,512]{1,0,2:T(4,128)(2,1)S(1)}, u32[]{:S(2)}, u32[]{:S(2)}) async-start(bf16[3,384,512]{1,0,2:T(4,128)(2,1)} %copy.50), calls=%async_computation | async-start | bytes 3145728 | tf_op jit(solution)/shard_map/all_to_all | solution.py:107
  43.4 2.5 %copy-start.11 = (f32[128,64,1]{0,1,2:T(8,128)S(1)}, f32[128,64,1]{0,1,2:T(8,128)}, u32[]{:S(2)}) copy-start(f32[128,64,1]{0,1,2:T(8,128)} %constant.107) | copy-start | bytes 98308
  45.9 1.4 copy-start.10
  47.4 1.5 copy-start
  47.4 1.5 copy-start.1
  47.4 1.5 copy-start.5
  49.8 1.0 copy-start.2
  87.8 1.4 copy-start.3
  87.8 1.9 %copy-start.4 = (f32[128,16,192]{0,2,1:T(8,128)S(1)}, f32[128,16,192]{0,2,1:T(8,128)}, u32[]{:S(2)}) copy-start(f32[128,16,192]{0,2,1:T(8,128)} %convolution_add_fusion) | copy-start | bytes 4718596
  93.7 0.9 copy-start.12
  94.7 1.3 copy-start.14
  96.0 1.6 copy-start.13
  100.9 1.9 %copy-start.6 = (f32[2,8,32,384]{3,1,2,0:T(8,128)S(1)}, f32[2,8,32,384]{3,1,2,0:T(8,128)}, u32[]{:S(2)}) copy-start(f32[2,8,32,384]{3,1,2,0:T(8,128)} %copy.66) | copy-start | bytes 2359300
  123.1 8.4 %collective-permute-start = (bf16[384,512]{0,1:T(8,128)(2,1)S(1)}, bf16[384,512]{0,1:T(8,128)(2,1)S(1)}, u32[]{:S(2)}, u32[]{:S(2)}) collective-permute-start(bf16[384,512]{0,1:T(8,128)(2,1)S(1)} %bitcast.133), channel_id=1, source_target_pairs={{0,1},{1,2},{2,3},{3,4},{4,5},{5,6},{6,7},{7,0},{8,9},{9,10},{10,1... | collective-permute-start | bytes 1179656 | tf_op jit(solution)/shard_map/ppermute | solution.py:20
  123.1 8.4 %collective-permute-start.1 = (bf16[384,512]{0,1:T(8,128)(2,1)S(1)}, bf16[384,512]{0,1:T(8,128)(2,1)S(1)}, u32[]{:S(2)}, u32[]{:S(2)}) collective-permute-start(bf16[384,512]{0,1:T(8,128)(2,1)S(1)} %bitcast.134), channel_id=1, source_target_pairs={{0,7},{1,0},{2,1},{3,2},{4,3},{5,4},{6,5},{7,6},{8,15},{9,8},{10,9... | collective-permute-start | bytes 1179656 | tf_op jit(solution)/shard_map/ppermute | solution.py:25
  131.5 8.4 %collective-permute-start.2 = (bf16[384,512]{0,1:T(8,128)(2,1)S(1)}, bf16[384,512]{0,1:T(8,128)(2,1)S(1)}, u32[]{:S(2)}, u32[]{:S(2)}) collective-permute-start(bf16[384,512]{0,1:T(8,128)(2,1)S(1)} %collective-permute-done), channel_id=1, source_target_pairs={{0,1},{1,2},{2,3},{3,4},{4,5},{5,6},{6,7},{7,0},{8,9},{9,10},{10,1... | collective-permute-start | bytes 1179656 | tf_op jit(solution)/shard_map/ppermute | solution.py:20
  131.5 8.8 %collective-permute-start.3 = (bf16[384,512]{0,1:T(8,128)(2,1)S(1)}, bf16[384,512]{0,1:T(8,128)(2,1)S(1)}, u32[]{:S(2)}, u32[]{:S(2)}) collective-permute-start(bf16[384,512]{0,1:T(8,128)(2,1)S(1)} %collective-permute-done.1), channel_id=1, source_target_pairs={{0,7},{1,0},{2,1},{3,2},{4,3},{5,4},{6,5},{7,6},{8,15},{9,8},{10,9... | collective-permute-start | bytes 1179656 | tf_op jit(solution)/shard_map/ppermute | solution.py:25
  139.9 8.4 %collective-permute-start.4 = (bf16[384,512]{0,1:T(8,128)(2,1)S(1)}, bf16[384,512]{0,1:T(8,128)(2,1)S(1)}, u32[]{:S(2)}, u32[]{:S(2)}) collective-permute-start(bf16[384,512]{0,1:T(8,128)(2,1)S(1)} %collective-permute-done.2), channel_id=1, source_target_pairs={{0,1},{1,2},{2,3},{3,4},{4,5},{5,6},{6,7},{7,0},{8,9},{9,10},{10,1... | collective-permute-start | bytes 1179656 | tf_op jit(solution)/shard_map/ppermute | solution.py:20
  140.3 8.3 %collective-permute-start.5 = (bf16[384,512]{0,1:T(8,128)(2,1)S(1)}, bf16[384,512]{0,1:T(8,128)(2,1)S(1)}, u32[]{:S(2)}, u32[]{:S(2)}) collective-permute-start(bf16[384,512]{0,1:T(8,128)(2,1)S(1)} %collective-permute-done.3), channel_id=1, source_target_pairs={{0,7},{1,0},{2,1},{3,2},{4,3},{5,4},{6,5},{7,6},{8,15},{9,8},{10,9... | collective-permute-start | bytes 1179656 | tf_op jit(solution)/shard_map/ppermute | solution.py:25
  143.3 13.5 %copy-start.15 = (bf16[4096,512]{1,0:T(8,128)(2,1)S(1)}, bf16[4096,512]{1,0:T(8,128)(2,1)}, u32[]{:S(2)}) copy-start(bf16[4096,512]{1,0:T(8,128)(2,1)} %param.21) | copy-start | bytes 12582916
  148.3 8.4 %collective-permute-start.6 = (bf16[384,512]{0,1:T(8,128)(2,1)S(1)}, bf16[384,512]{0,1:T(8,128)(2,1)S(1)}, u32[]{:S(2)}, u32[]{:S(2)}) collective-permute-start(bf16[384,512]{0,1:T(8,128)(2,1)S(1)} %collective-permute-done.4), channel_id=1, source_target_pairs={{0,1},{1,2},{2,3},{3,4},{4,5},{5,6},{6,7},{7,0},{8,9},{9,10},{10,1... | collective-permute-start | bytes 1179656 | tf_op jit(solution)/shard_map/ppermute | solution.py:20
